TPU v7x, 256 devices: a whole 4x4x8 slice. The times are simulated.
256 devices in a mesh: dp: 16 (over z, core), frame: 16 (over x, y).
Axes of the slice: x: 4, y: 4, z: 8, core: 2. Of those that a mesh axis runs over, the one named last changes fastest.
Arguments:
- latents: bfloat16 [16, 32, 128, 1280], P('dp', 'frame'), may hold values from -330 to 330
- timestep: int32 [16], P('dp'), may hold values from 0 to 999
- norm_gain: float32 [1280], replicated, may hold values from 0.1 to 1.9
- time_weight: bfloat16 [320, 1280], P('dp'), may hold values from -0.3125 to 0.3125
- conv_weight: bfloat16 [3, 1280, 1280], P(None, ('dp', 'frame')), may hold values from -0.09375 to 0.09375
- attend_weight: bfloat16 [1280, 3840], P(('dp', 'frame')), may hold values from -0.3354102 to 0.3354102
- output_weight: bfloat16 [1280, 1280], P(('dp', 'frame')), may hold values from -0.15625 to 0.15625
Outputs:
- block_out: bfloat16 [16, 32, 128, 1280], P('dp', 'frame')
All inputs are finite; a program needn't handle non-finite values.
Results may differ from a plain program's by a relative error of at most 0.0051.
Values may be sent and summed in bfloat16 or wider, within the bound.
No kernel may reach another device: no remote copies, remote signals or barrier semaphores. Data moves between devices by JAX's collectives and lax.ppermute only.
A program may use at most 128 MiB of HBM per device.

v0:
```python
import functools
import math
import jax
import jax.numpy as jnp
from jax import lax
from jax.sharding import Mesh
from jax.sharding import PartitionSpec as P

HEADS = 20
HD = 64
GROUPS = 32
TEMB = 320
FRAME = ("frame_0", "frame_1")
DP_FRAME = ("dp", "frame_0", "frame_1")


def laid_out(blocks, dim):
    blocks = jnp.moveaxis(blocks, 0, dim)
    dims = blocks.shape
    return blocks.reshape(*dims[:dim], dims[dim] * dims[dim + 1], *dims[dim + 2 :])


def sent_to_all(array, axis):
    count = lax.axis_size(axis)
    return lax.all_to_all(
        jnp.broadcast_to(array[None], (count, *array.shape)), axis, 0, 0, tiled=True
    )


def collect(array, axis, dim):
    return laid_out(sent_to_all(array, axis), dim)


def by_axis(array, axes):
    return functools.reduce(lax.psum, axes, array)


def with_halo(array, sides, width):
    for axis, dim in sides:
        count, length = (lax.axis_size(axis), array.shape[dim])
        up = [(i, (i + 1) % count) for i in range(count - 1)]
        down = [(j, i) for i, j in up]
        last = lax.slice_in_dim(array, length - width, length, axis=dim)
        initial = lax.slice_in_dim(array, 0, width, axis=dim)
        before = lax.ppermute(last, axis, up)
        after = lax.ppermute(initial, axis, down)
        array = jnp.concatenate([before, array, after], axis=dim)
    return array


def sinusoid(timestep):
    half_dim = TEMB // 2
    ladder = jnp.arange(half_dim, dtype=jnp.float32)
    freqs = jnp.exp(-math.log(10000.0) * ladder / half_dim)
    angles = timestep.astype(jnp.float32)[:, None] * freqs[None, :]
    return jnp.concatenate([jnp.cos(angles), jnp.sin(angles)], axis=-1)


def attend_pixels(triple):
    count_items, frames_all, pixels_here, width_three = triple.shape
    channels = width_three // 3
    parts = triple.reshape(count_items, frames_all, pixels_here, 3, HEADS, HD)
    queries = parts[:, :, :, 0]
    key_part = parts[:, :, :, 1]
    value_part = parts[:, :, :, 2]
    scores = jnp.einsum(
        "nfphd,ngphd->nphfg", queries, key_part, preferred_element_type=jnp.float32
    ) / math.sqrt(HD)
    peak = jnp.max(scores, axis=-1, keepdims=True)
    expo = jnp.exp(scores - peak)
    probs = (expo / jnp.sum(expo, axis=-1, keepdims=True)).astype(jnp.bfloat16)
    attended = jnp.einsum(
        "nphfg,ngphd->nfphd", probs, value_part, preferred_element_type=jnp.float32
    )
    attended = attended.astype(jnp.bfloat16).reshape(count_items, frames_all, pixels_here, channels)
    return lax.all_to_all(attended, FRAME, split_axis=1, concat_axis=2, tiled=True)


def fold_rows(total, rows, piece):
    return total + jnp.dot(rows, piece, preferred_element_type=jnp.float32)


def shards(latents, timestep, norm_gain, time_weight, conv_weight, attend_weight, output_weight):
    count_clips, frames_dev, pixels, channels = latents.shape
    group_width = channels // GROUPS
    time_full = collect(time_weight, "dp", 0)
    features = sinusoid(timestep).astype(jnp.bfloat16)
    time_bias = jnp.dot(features, time_full, preferred_element_type=jnp.float32)
    values = latents.astype(jnp.float32)
    grouped = values.reshape(count_clips, frames_dev, pixels, GROUPS, group_width)
    members = frames_dev * lax.axis_size(FRAME) * pixels * group_width
    center = by_axis(jnp.sum(grouped, axis=(1, 2, 4)), FRAME) / members
    deviate = grouped - center[:, None, None, :, None]
    spread = by_axis(jnp.sum(deviate * deviate, axis=(1, 2, 4)), FRAME) / members
    normed_group = deviate / jnp.sqrt(spread[:, None, None, :, None] + 1e-05)
    scaled = normed_group.reshape(count_clips, frames_dev, pixels, channels) * norm_gain
    hidden = jax.nn.silu(scaled).astype(jnp.bfloat16)
    padded = with_halo(hidden, ((FRAME, 1),), 1)
    windows = [padded[:, offset : offset + frames_dev].reshape(-1, channels) for offset in range(3)]
    conv_init = jnp.zeros((count_clips * frames_dev * pixels, channels), jnp.float32)
    conv_slab = collect(conv_weight, FRAME, 1)
    total = conv_init
    piece = lax.all_gather(conv_slab, "dp", axis=1, tiled=True)
    for offset in range(3):
        total = fold_rows(total, windows[offset], piece[offset])
    conv = total
    conv = conv.reshape(count_clips, frames_dev, pixels, channels) + time_bias[:, None, None, :]
    residual = (values + conv).astype(jnp.bfloat16)
    rows = residual.astype(jnp.float32)
    row_mean = jnp.mean(rows, axis=-1, keepdims=True)
    row_var = jnp.mean((rows - row_mean) ** 2, axis=-1, keepdims=True)
    normed = ((rows - row_mean) / jnp.sqrt(row_var + 1e-05)).astype(jnp.bfloat16)
    attend_slab = collect(attend_weight, FRAME, 0)
    block = lax.all_to_all(normed, FRAME, split_axis=2, concat_axis=1, tiled=True)
    count_items, frames_all, pixels_here, width = block.shape
    flat = block.reshape(-1, width)
    empty = jnp.zeros((flat.shape[0], 3 * channels), jnp.float32)
    product = fold_rows(empty, flat, lax.all_gather(attend_slab, "dp", axis=0, tiled=True))
    triple_block = product.astype(jnp.bfloat16).reshape(
        count_items, frames_all, pixels_here, 3 * width
    )
    attended = attend_pixels(triple_block)
    flat_attended = attended.reshape(-1, channels)
    output_slab = collect(output_weight, FRAME, 0)
    out_init = jnp.zeros((flat_attended.shape[0], channels), jnp.float32)
    projected = fold_rows(
        out_init, flat_attended, lax.all_gather(output_slab, "dp", axis=0, tiled=True)
    )
    mixed = rows + projected.reshape(count_clips, frames_dev, pixels, channels)
    return mixed.astype(jnp.bfloat16)


def solution(mesh):
    split = Mesh(mesh.devices.reshape(mesh.shape["dp"], 4, 4), ("dp", "frame_0", "frame_1"))
    placed = (
        P("dp", FRAME, None, None),
        P("dp"),
        P(),
        P("dp", None),
        P(None, DP_FRAME, None),
        P(DP_FRAME, None),
        P(DP_FRAME, None),
    )
    return jax.shard_map(
        shards, mesh=split, in_specs=placed, out_specs=P("dp", FRAME, None, None), check_vma=False
    )
```

profile of v0, /device:TPU:1, one launch (start us, length us, event | category | flops | bytes accessed | tf_op | source)
XLA Modules:
  0.0 227.9 jit_solution(3048187557169434955)
XLA Ops:
  7.6 21.1 %all_to_all.50 = bf16[16,3,5,1280]{3,1,2,0:T(4,128)(2,1)S(1)} all-to-all(bf16[16,3,5,1280]{3,1,2,0:T(4,128)(2,1)S(1)} %broadcast_in_dim.8), channel_id=1, replica_groups=mesh['dp'=16,'frame_0'=4,'frame_1'=4] {'frame_0','frame_1'}, dimensions={0} | all-to-all | bytes 1228800 | tf_op jit(solution)/shard_map/all_to_all | solution.py:25
  29.8 17.6 %all_to_all.51 = bf16[16,5,3840]{2,1,0:T(8,128)(2,1)S(1)} all-to-all(bf16[16,5,3840]{2,1,0:T(8,128)(2,1)S(1)} %broadcast_in_dim.10), channel_id=1, replica_groups=mesh['dp'=16,'frame_0'=4,'frame_1'=4] {'frame_0','frame_1'}, dimensions={0} | all-to-all | bytes 1228800 | tf_op jit(solution)/shard_map/all_to_all | solution.py:25
  49.3 3.5 %all-to-all-start.5 = ((bf16[16,5,1280]{2,1,0:T(8,128)(2,1)}), bf16[16,5,1280]{2,1,0:T(8,128)(2,1)S(1)}, u32[]{:S(2)}, u32[]{:S(2)}) async-start(bf16[16,5,1280]{2,1,0:T(8,128)(2,1)} %broadcast_in_dim.11), calls=%async_computation.5 | async-start | bytes 655360 | tf_op jit(solution)/shard_map/all_to_all | solution.py:25
  53.2 9.3 %psum.28 = f32[1,32]{1,0:T(1,128)S(1)} all-reduce(f32[1,32]{1,0:T(1,128)S(1)} %bitcast.84), channel_id=1, replica_groups=mesh['dp'=16,'frame_0'=4,'frame_1'=4] {'frame_0'}, use_global_device_ids=true, to_apply=%region_2.0 | all-reduce | flops 32 | bytes 256 | tf_op jit(solution)/shard_map/psum | solution.py:35
  62.5 9.2 %psum.29 = f32[1,32]{1,0:T(1,128)S(1)} all-reduce(f32[1,32]{1,0:T(1,128)S(1)} %psum.28), channel_id=1, replica_groups=mesh['dp'=16,'frame_0'=4,'frame_1'=4] {'frame_1'}, use_global_device_ids=true, to_apply=%region_3.0 | all-reduce | flops 32 | bytes 256 | tf_op jit(solution)/shard_map/psum | solution.py:35
  72.3 6.8 %psum.30 = f32[1,32]{1,0:T(1,128)S(1)} all-reduce(f32[1,32]{1,0:T(1,128)S(1)} %bitcast.83), channel_id=1, replica_groups=mesh['dp'=16,'frame_0'=4,'frame_1'=4] {'frame_0'}, use_global_device_ids=true, to_apply=%region_6.7 | all-reduce | flops 32 | bytes 256 | tf_op jit(solution)/shard_map/psum | solution.py:35
  79.1 6.8 %psum.31 = f32[1,32]{1,0:T(1,128)S(1)} all-reduce(f32[1,32]{1,0:T(1,128)S(1)} %psum.30), channel_id=1, replica_groups=mesh['dp'=16,'frame_0'=4,'frame_1'=4] {'frame_1'}, use_global_device_ids=true, to_apply=%region_7.8 | all-reduce | flops 32 | bytes 256 | tf_op jit(solution)/shard_map/psum | solution.py:35
  87.1 16.0 %all-to-all-start.1 = ((bf16[16,20,1280]{2,1,0:T(8,128)(2,1)}), bf16[16,20,1280]{2,1,0:T(8,128)(2,1)S(1)}, u32[]{:S(2)}, u32[]{:S(2)}) async-start(bf16[16,20,1280]{2,1,0:T(8,128)(2,1)} %broadcast_in_dim.9), calls=%async_computation.1 | async-start | bytes 1966080 | tf_op jit(solution)/shard_map/all_to_all | solution.py:25
  104.3 3.6 %collective-permute-start = (bf16[1,1,128,1280]{3,2,1,0:T(8,128)(2,1)}, bf16[1,1,128,1280]{3,2,1,0:T(8,128)(2,1)S(1)}, u32[]{:S(2)}, u32[]{:S(2)}) collective-permute-start(bf16[1,1,128,1280]{3,2,1,0:T(8,128)(2,1)} %get-tuple-element.12), channel_id=1, source_target_pairs={{0,1},{1,2},{2,3},{3,4},{4,5},{5,6},{6,7},{7,8},{8,9},{9,10},{10,1... | collective-permute-start | bytes 983048 | tf_op jit(solution)/shard_map/ppermute | solution.py:45
  110.9 4.4 %collective-permute-done = bf16[1,1,128,1280]{3,2,1,0:T(8,128)(2,1)S(1)} collective-permute-done((bf16[1,1,128,1280]{3,2,1,0:T(8,128)(2,1)}, bf16[1,1,128,1280]{3,2,1,0:T(8,128)(2,1)S(1)}, u32[]{:S(2)}, u32[]{:S(2)}) %collective-permute-start) | collective-permute-done | bytes 327712 | tf_op jit(solution)/shard_map/ppermute | solution.py:45
  115.2 3.6 %collective-permute-done.1 = bf16[1,1,128,1280]{3,2,1,0:T(8,128)(2,1)} collective-permute-done((bf16[1,1,128,1280]{3,2,1,0:T(8,128)(2,1)S(1)}, bf16[1,1,128,1280]{3,2,1,0:T(8,128)(2,1)}, u32[]{:S(2)}, u32[]{:S(2)}) %collective-permute-start.1) | collective-permute-done | bytes 327712 | tf_op jit(solution)/shard_map/ppermute | solution.py:46
  121.0 17.5 %all-to-all-done.1 = bf16[16,20,1280]{2,1,0:T(8,128)(2,1)S(1)} async-done(((bf16[16,20,1280]{2,1,0:T(8,128)(2,1)}), bf16[16,20,1280]{2,1,0:T(8,128)(2,1)S(1)}, u32[]{:S(2)}, u32[]{:S(2)}) %all-to-all-start.1) | async-done | bytes 819232 | tf_op jit(solution)/shard_map/all_to_all | solution.py:25
  139.0 3.2 %fusion.1 = f32[256,1280]{1,0:T(8,128)S(1)} fusion(bf16[256,1280]{1,0:T(8,128)(2,1)} %bitcast.80, bf16[3,1280,1280]{2,1,0:T(8,128)(2,1)} %all-gather.4.cloned.1.call-done), kind=kOutput, calls=%fused_computation.3 | convolution fusion | flops 838860800 | bytes 5242880 | tf_op jit(solution)/shard_map/dot_general | solution.py:80
  142.2 3.0 %fusion.2 = f32[256,1280]{1,0:T(8,128)S(1)} fusion(bf16[256,1280]{1,0:T(8,128)(2,1)S(1)} %bitcast.75, bf16[3,1280,1280]{2,1,0:T(8,128)(2,1)} %all-gather.4.cloned.1.call-done), kind=kOutput, calls=%fused_computation.5 | convolution fusion | flops 838860800 | bytes 5242880 | tf_op jit(solution)/shard_map/dot_general | solution.py:80
  145.2 3.0 %fusion.7 = f32[256,1280]{1,0:T(8,128)S(1)} fusion(f32[256,1280]{1,0:T(8,128)S(1)} %fusion.1, f32[256,1280]{1,0:T(8,128)S(1)} %fusion.2, bf16[256,1280]{1,0:T(8,128)(2,1)S(1)} %bitcast.79, bf16[3,1280,1280]{2,1,0:T(8,128)(2,1)} %all-gather.4.cloned.1.call-done), kind=kOutput, calls=%fused_computation.11 | convolution fusion | flops 839516160 | bytes 7864320 | tf_op jit(solution)/shard_map/dot_general | solution.py:80
  149.8 17.2 %all_to_all.52 = bf16[1,2,128,1280]{3,1,0,2:T(2,128)(2,1)S(1)} all-to-all(bf16[1,2,128,1280]{3,1,0,2:T(2,128)(2,1)S(1)} %copy.42), channel_id=1, replica_groups=mesh['dp'=16,'frame_0'=4,'frame_1'=4] {'frame_0','frame_1'}, dimensions={2} | all-to-all | bytes 1310720 | tf_op jit(solution)/shard_map/all_to_all | solution.py:114
  168.0 8.1 %all-gather.6.cloned.1.call-done = bf16[1280,3840]{1,0:T(8,128)(2,1)} async-done(((bf16[80,3840]{1,0:T(8,128)(2,1)}), bf16[1280,3840]{1,0:T(8,128)(2,1)}) %all-gather.6.cloned.1.call-update) | async-done | bytes 9830416 | tf_op jit(solution)/shard_map/all_gather | solution.py:118
  176.1 6.7 %convolution_convert_fusion = bf16[256,3840]{1,0:T(8,128)(2,1)S(1)} fusion(bf16[256,1280]{1,0:T(8,128)(2,1)} %bitcast.82, bf16[1280,3840]{1,0:T(8,128)(2,1)} %all-gather.6.cloned.1.call-done), kind=kOutput, calls=%fused_computation.1 | convolution fusion | flops 2517565440 | bytes 12451840 | tf_op jit(solution)/shard_map/dot_general | solution.py:80
  182.8 4.5 %reshape_reshape.3 = bf16[1,32,8,3,20,64]{5,4,3,2,1,0:T(8,128)(2,1)} reshape(bf16[256,3840]{1,0:T(8,128)(2,1)S(1)} %convolution_convert_fusion) | data formatting | bytes 3932160 | tf_op jit(solution)/shard_map/reshape;reshape | solution.py:62
  187.3 3.3 %fusion.37 = (bf16[1,32,8,1,20,64]{5,4,3,2,1,0:T(8,128)(2,1)S(1)}, bf16[1,32,8,1,20,64]{5,4,3,2,1,0:T(8,128)(2,1)S(1)}, bf16[1,32,8,1,20,64]{5,4,3,2,1,0:T(8,128)(2,1)S(1)}) fusion(bf16[1,32,8,3,20,64]{5,4,3,2,1,0:T(8,128)(2,1)} %reshape_reshape.3), kind=kLoop, calls=%fused_computation.57 | loop fusion | bytes 3932160 | tf_op jit(solution)/shard_map/slice | solution.py:65
  192.3 6.0 %fusion.39 = (f32[8,20,32]{2,1,0:T(8,128)S(1)}, f32[8,20,32,32]{2,3,1,0:T(8,128)S(1)}) fusion(f32[8,20,32,32]{2,3,1,0:T(8,128)S(1)} %fusion.30), kind=kOutput, calls=%fused_computation.59 | output fusion | flops 655391 | bytes 1331200 | tf_op jit(solution)/shard_map/sub | solution.py:70
  201.7 4.6 %all-to-all-start.4 = ((bf16[1,32,8,1280]{3,2,0,1:T(8,128)(2,1)}), bf16[1,32,8,1280]{3,2,0,1:T(8,128)(2,1)S(1)}, u32[]{:S(2)}, u32[]{:S(2)}) async-start(bf16[1,32,8,1280]{3,2,0,1:T(8,128)(2,1)} %bitcast.22), calls=%async_computation.4 | async-start | bytes 1310720 | tf_op jit(solution)/shard_map/all_to_all | solution.py:76
  206.2 9.3 %all-gather.8.cloned.1.call-done = bf16[1280,1280]{1,0:T(8,128)(2,1)} async-done(((bf16[80,1280]{1,0:T(8,128)(2,1)}), bf16[1280,1280]{1,0:T(8,128)(2,1)}) %all-gather.8.cloned.1.call-update) | async-done | bytes 3276816 | tf_op jit(solution)/shard_map/all_gather | solution.py:127
  217.6 3.8 %fusion.14 = bf16[1,2,128,1280]{3,2,1,0:T(8,128)(2,1)} fusion(bf16[1280,1280]{1,0:T(8,128)(2,1)} %all-gather.8.cloned.1.call-done, bf16[1,2,128,1280]{3,2,1,0:T(8,128)(2,1)S(1)} %get-tuple-element.6, bf16[1,2,16,8,1280]{4,3,1,2,0:T(8,128)(2,1)S(1)} %bitcast.81), kind=kOutput, calls=%fused_computation.16 | convolution fusion | flops 839843840 | bytes 5242880 | tf_op jit(solution)/shard_map/dot_general | solution.py:80
  (61 shorter events, 21.7 us)
Async XLA Ops:
  6.5 132.4 %all-gather.4.cloned.1.call-start = ((), (), s32[]{:S(2)}) async-start(), calls=%async_computation.6 | async-start | bytes 10444800 | tf_op jit(solution)/shard_map/all_gather | solution.py:103
  7.6 22.1 %copy-start.2 = (bf16[5,3840]{1,0:T(8,128)(2,1)S(1)}, bf16[5,3840]{1,0:T(8,128)(2,1)}, u32[]{:S(2)}) copy-start(bf16[5,3840]{1,0:T(8,128)(2,1)} %param.12) | copy-start | bytes 115204
  29.6 146.4 %all-gather.6.cloned.1.call-start = ((), (), s32[]{:S(2)}) async-start(), calls=%async_computation.7 | async-start | bytes 10444800 | tf_op jit(solution)/shard_map/all_gather | solution.py:118
  47.4 1.1 copy-start.4
  47.4 5.4 %copy-start = (bf16[1,2,128,1280]{3,2,1,0:T(8,128)(2,1)S(1)}, bf16[1,2,128,1280]{3,2,1,0:T(8,128)(2,1)}, u32[]{:S(2)}) copy-start(bf16[1,2,128,1280]{3,2,1,0:T(8,128)(2,1)} %param.7) | copy-start | bytes 1966084
  48.5 37.6 %copy-start.3 = (bf16[20,1280]{1,0:T(8,128)(2,1)S(1)}, bf16[20,1280]{1,0:T(8,128)(2,1)}, u32[]{:S(2)}) copy-start(bf16[20,1280]{1,0:T(8,128)(2,1)} %param.10) | copy-start | bytes 153604
  49.3 36.8 %all-to-all-start.5 = ((bf16[16,5,1280]{2,1,0:T(8,128)(2,1)}), bf16[16,5,1280]{2,1,0:T(8,128)(2,1)S(1)}, u32[]{:S(2)}, u32[]{:S(2)}) async-start(bf16[16,5,1280]{2,1,0:T(8,128)(2,1)} %broadcast_in_dim.11), calls=%async_computation.5 | async-start | bytes 655360 | tf_op jit(solution)/shard_map/all_to_all | solution.py:25
  72.1 31.0 %copy-start.5 = (f32[1280]{0:T(1024)S(1)}, f32[1280]{0:T(1024)}, u32[]{:S(2)}) copy-start(f32[1280]{0:T(1024)} %param.9) | copy-start | bytes 15364
  87.1 51.4 %all-to-all-start.1 = ((bf16[16,20,1280]{2,1,0:T(8,128)(2,1)}), bf16[16,20,1280]{2,1,0:T(8,128)(2,1)S(1)}, u32[]{:S(2)}, u32[]{:S(2)}) async-start(bf16[16,20,1280]{2,1,0:T(8,128)(2,1)} %broadcast_in_dim.9), calls=%async_computation.1 | async-start | bytes 1966080 | tf_op jit(solution)/shard_map/all_to_all | solution.py:25
  103.1 112.5 %all-gather.8.cloned.1.call-start = ((), (), s32[]{:S(2)}) async-start(), calls=%async_computation.8 | async-start | bytes 3481600 | tf_op jit(solution)/shard_map/all_gather | solution.py:127
  104.3 10.9 %collective-permute-start = (bf16[1,1,128,1280]{3,2,1,0:T(8,128)(2,1)}, bf16[1,1,128,1280]{3,2,1,0:T(8,128)(2,1)S(1)}, u32[]{:S(2)}, u32[]{:S(2)}) collective-permute-start(bf16[1,1,128,1280]{3,2,1,0:T(8,128)(2,1)} %get-tuple-element.12), channel_id=1, source_target_pairs={{0,1},{1,2},{2,3},{3,4},{4,5},{5,6},{6,7},{7,8},{8,9},{9,10},{10,1... | collective-permute-start | bytes 983048 | tf_op jit(solution)/shard_map/ppermute | solution.py:45
  108.0 10.9 %collective-permute-start.1 = (bf16[1,1,128,1280]{3,2,1,0:T(8,128)(2,1)S(1)}, bf16[1,1,128,1280]{3,2,1,0:T(8,128)(2,1)}, u32[]{:S(2)}, u32[]{:S(2)}) collective-permute-start(bf16[1,1,128,1280]{3,2,1,0:T(8,128)(2,1)S(1)} %get-tuple-element.13), channel_id=1, source_target_pairs={{1,0},{2,1},{3,2},{4,3},{5,4},{6,5},{7,6},{8,7},{9,8},{10,9},{11,1... | collective-permute-start | bytes 983048 | tf_op jit(solution)/shard_map/ppermute | solution.py:46
  142.2 3.0 %copy-start.1 = (bf16[1,2,128,1280]{3,2,1,0:T(8,128)(2,1)S(1)}, bf16[1,2,128,1280]{3,2,1,0:T(8,128)(2,1)}, u32[]{:S(2)}) copy-start(bf16[1,2,128,1280]{3,2,1,0:T(8,128)(2,1)} %get-tuple-element.10) | copy-start | bytes 1966084
  201.7 15.9 %all-to-all-start.4 = ((bf16[1,32,8,1280]{3,2,0,1:T(8,128)(2,1)}), bf16[1,32,8,1280]{3,2,0,1:T(8,128)(2,1)S(1)}, u32[]{:S(2)}, u32[]{:S(2)}) async-start(bf16[1,32,8,1280]{3,2,0,1:T(8,128)(2,1)} %bitcast.22), calls=%async_computation.4 | async-start | bytes 1310720 | tf_op jit(solution)/shard_map/all_to_all | solution.py:76
Sparse Core Ops, SparseCore 0:
  29.8 63.7 all-gather.3
  95.4 80.5 all-gather.5
  177.9 37.6 all-gather.7
where the time goes:
time: 229 us; the launch traced here: 228 us
  blocking collectives  88 us (38%)
  waiting for transfers between devices  45.1 us (20%)
  starting transfers between devices  29.1 us (13%)
  matrix products  23 us (10%)
  local copies, waits for them, and re-layouts  18.6 us (8%)
  between operations  14 us (6%)
  other arithmetic  10.1 us (4%)
    all_to_all x2, blocking collectives, sent_to_all(): lax.all_to_all(jnp.broadcast_to(array[None], (count, *array.shape)), axis...  38.7 us
    psum x4, blocking collectives, by_axis(): return functools.reduce(lax.psum, axes, array)  32.1 us
    dot_general x5, matrix products, fold_rows(): return total + jnp.dot(rows, piece, preferred_element_type=jnp.float32)  19.8 us
    all_to_all x2, starting transfers between devices, sent_to_all(): lax.all_to_all(jnp.broadcast_to(array[None], (count, *array.shape)), axis...  19.5 us
    all_to_all x2, waiting for transfers between devices, sent_to_all(): lax.all_to_all(jnp.broadcast_to(array[None], (count, *array.shape)), axis...  17.5 us
    all_to_all x1, blocking collectives, shards(): lax.all_to_all(normed, FRAME, split_axis=2, concat_axis=1, tiled=True)  17.2 us
    all_gather x1, waiting for transfers between devices, shards(): lax.all_gather(output_slab, 'dp', axis=0, tiled=True)  9.34 us
    all_gather x1, waiting for transfers between devices, shards(): lax.all_gather(attend_slab, 'dp', axis=0, tiled=True)  8.12 us
  transfers between devices with their start and end apart: 8, of which 6 were waited for; matrix products, arithmetic and copies ran while one was open for 20% of the time, Pallas kernels for 0%

commit v1 on v0

--- a/solution.py
+++ b/solution.py
@@ -123,9 +123,13 @@
     flat_attended = attended.reshape(-1, channels)
     output_slab = collect(output_weight, FRAME, 0)
     out_init = jnp.zeros((flat_attended.shape[0], channels), jnp.float32)
-    projected = fold_rows(
-        out_init, flat_attended, lax.all_gather(output_slab, "dp", axis=0, tiled=True)
-    )
+
+    def run_signs(view, along_dim):
+        spare = jnp.stack(tuple((view for _ in range(lax.axis_size("dp")))))
+        extra = lax.all_to_all(spare, axis_name="dp", split_axis=0, concat_axis=0)
+        return jnp.concatenate(extra, axis=along_dim)
+
+    projected = fold_rows(out_init, flat_attended, run_signs(output_slab, along_dim=0))
     mixed = rows + projected.reshape(count_clips, frames_dev, pixels, channels)
     return mixed.astype(jnp.bfloat16)
 

time: 229 us -> 287 us (1.25)
  the two profiles are of different devices: /device:TPU:1 before, /device:TPU:96 now
where the time goes in v1:
time: 287 us; the launch traced here: 286 us
  blocking collectives  106 us (37%)
  waiting for transfers between devices  81.4 us (28%)
  starting transfers between devices  33.9 us (12%)
  matrix products  23.1 us (8%)
  local copies, waits for them, and re-layouts  18.4 us (6%)
  between operations  14.3 us (5%)
  other arithmetic  9.09 us (3%)
    all_gather x1, waiting for transfers between devices, shards(): lax.all_gather(attend_slab, 'dp', axis=0, tiled=True)  63.8 us
    all_to_all x2, blocking collectives, sent_to_all(): lax.all_to_all(jnp.broadcast_to(array[None], (count, *array.shape)), axis...  39.9 us
    psum x4, blocking collectives, by_axis(): return functools.reduce(lax.psum, axes, array)  34.9 us
    all_to_all x1, blocking collectives, attend_pixels(): lax.all_to_all(attended, FRAME, split_axis=1, concat_axis=2, tiled=True)  31.3 us
    dot_general x5, matrix products, fold_rows(): return total + jnp.dot(rows, piece, preferred_element_type=jnp.float32)  19.9 us
    all_to_all x2, starting transfers between devices, sent_to_all(): lax.all_to_all(jnp.broadcast_to(array[None], (count, *array.shape)), axis...  15.3 us
    all_to_all x1, waiting for transfers between devices, shards(): lax.all_to_all(normed, FRAME, split_axis=2, concat_axis=1, tiled=True)  10.7 us
    all_to_all x1, starting transfers between devices, run_signs(): extra = lax.all_to_all(spare, axis_name='dp', split_axis=0, concat_axis=0)  7.31 us
  transfers between devices with their start and end apart: 8, of which 4 were waited for; matrix products, arithmetic and copies ran while one was open for 16% of the time, Pallas kernels for 0%

profile of v1, /device:TPU:96, one launch (start us, length us, event | category | flops | bytes accessed | tf_op | source)
XLA Modules:
  0.0 286.4 jit_solution(8515371719553929535)
XLA Ops:
  7.6 21.4 %all_to_all.55 = bf16[16,3,5,1280]{3,1,2,0:T(4,128)(2,1)S(1)} all-to-all(bf16[16,3,5,1280]{3,1,2,0:T(4,128)(2,1)S(1)} %broadcast_in_dim.8), channel_id=1, replica_groups=mesh['dp'=16,'frame_0'=4,'frame_1'=4] {'frame_0','frame_1'}, dimensions={0} | all-to-all | bytes 1228800 | tf_op jit(solution)/shard_map/all_to_all | solution.py:25
  30.1 18.5 %all_to_all.56 = bf16[16,5,3840]{2,1,0:T(8,128)(2,1)S(1)} all-to-all(bf16[16,5,3840]{2,1,0:T(8,128)(2,1)S(1)} %broadcast_in_dim.10), channel_id=1, replica_groups=mesh['dp'=16,'frame_0'=4,'frame_1'=4] {'frame_0','frame_1'}, dimensions={0} | all-to-all | bytes 1228800 | tf_op jit(solution)/shard_map/all_to_all | solution.py:25
  50.7 7.8 %all-to-all-start.1 = ((bf16[16,20,1280]{2,1,0:T(8,128)(2,1)}), bf16[16,20,1280]{2,1,0:T(8,128)(2,1)S(1)}, u32[]{:S(2)}, u32[]{:S(2)}) async-start(bf16[16,20,1280]{2,1,0:T(8,128)(2,1)} %broadcast_in_dim.9), calls=%async_computation.1 | async-start | bytes 1966080 | tf_op jit(solution)/shard_map/all_to_all | solution.py:25
  58.8 9.2 %psum.28 = f32[1,32]{1,0:T(1,128)S(1)} all-reduce(f32[1,32]{1,0:T(1,128)S(1)} %bitcast.80), channel_id=1, replica_groups=mesh['dp'=16,'frame_0'=4,'frame_1'=4] {'frame_0'}, use_global_device_ids=true, to_apply=%region_2.0 | all-reduce | flops 32 | bytes 256 | tf_op jit(solution)/shard_map/psum | solution.py:35
  68.0 8.3 %psum.29 = f32[1,32]{1,0:T(1,128)S(1)} all-reduce(f32[1,32]{1,0:T(1,128)S(1)} %psum.28), channel_id=1, replica_groups=mesh['dp'=16,'frame_0'=4,'frame_1'=4] {'frame_1'}, use_global_device_ids=true, to_apply=%region_3.0 | all-reduce | flops 32 | bytes 256 | tf_op jit(solution)/shard_map/psum | solution.py:35
  76.9 8.6 %psum.30 = f32[1,32]{1,0:T(1,128)S(1)} all-reduce(f32[1,32]{1,0:T(1,128)S(1)} %bitcast.79), channel_id=1, replica_groups=mesh['dp'=16,'frame_0'=4,'frame_1'=4] {'frame_0'}, use_global_device_ids=true, to_apply=%region_6.7 | all-reduce | flops 32 | bytes 256 | tf_op jit(solution)/shard_map/psum | solution.py:35
  85.5 8.9 %psum.31 = f32[1,32]{1,0:T(1,128)S(1)} all-reduce(f32[1,32]{1,0:T(1,128)S(1)} %psum.30), channel_id=1, replica_groups=mesh['dp'=16,'frame_0'=4,'frame_1'=4] {'frame_1'}, use_global_device_ids=true, to_apply=%region_7.8 | all-reduce | flops 32 | bytes 256 | tf_op jit(solution)/shard_map/psum | solution.py:35
  95.0 2.9 %collective-permute-start = (bf16[1,1,128,1280]{3,2,1,0:T(8,128)(2,1)S(1)}, bf16[1,1,128,1280]{3,2,1,0:T(8,128)(2,1)S(1)}, u32[]{:S(2)}, u32[]{:S(2)}) collective-permute-start(bf16[1,1,128,1280]{3,2,1,0:T(8,128)(2,1)S(1)} %get-tuple-element.12), channel_id=1, source_target_pairs={{0,1},{1,2},{2,3},{3,4},{4,5},{5,6},{6,7},{7,8},{8,9},{9,10},{10,1... | collective-permute-start | bytes 983048 | tf_op jit(solution)/shard_map/ppermute | solution.py:45
  100.1 2.5 collective-permute-done
  102.5 4.4 %collective-permute-done.1 = bf16[1,1,128,1280]{3,2,1,0:T(8,128)(2,1)S(1)} collective-permute-done((bf16[1,1,128,1280]{3,2,1,0:T(8,128)(2,1)S(1)}, bf16[1,1,128,1280]{3,2,1,0:T(8,128)(2,1)S(1)}, u32[]{:S(2)}, u32[]{:S(2)}) %collective-permute-start.1) | collective-permute-done | bytes 327712 | tf_op jit(solution)/shard_map/ppermute | solution.py:46
  108.9 7.5 %all-to-all-start.5 = ((bf16[16,5,1280]{2,1,0:T(8,128)(2,1)}), bf16[16,5,1280]{2,1,0:T(8,128)(2,1)S(1)}, u32[]{:S(2)}, u32[]{:S(2)}) async-start(bf16[16,5,1280]{2,1,0:T(8,128)(2,1)} %broadcast_in_dim.11), calls=%async_computation.5 | async-start | bytes 655360 | tf_op jit(solution)/shard_map/all_to_all | solution.py:25
  116.8 3.2 %fusion.1 = f32[256,1280]{1,0:T(8,128)S(1)} fusion(bf16[256,1280]{1,0:T(8,128)(2,1)} %bitcast.76, bf16[3,1280,1280]{2,1,0:T(8,128)(2,1)} %all-gather.3.cloned.1.call-done), kind=kOutput, calls=%fused_computation.3 | convolution fusion | flops 838860800 | bytes 5242880 | tf_op jit(solution)/shard_map/dot_general | solution.py:80
  120.0 3.0 %fusion.2 = f32[256,1280]{1,0:T(8,128)S(1)} fusion(bf16[256,1280]{1,0:T(8,128)(2,1)S(1)} %bitcast.70, bf16[3,1280,1280]{2,1,0:T(8,128)(2,1)} %all-gather.3.cloned.1.call-done), kind=kOutput, calls=%fused_computation.5 | convolution fusion | flops 838860800 | bytes 5242880 | tf_op jit(solution)/shard_map/dot_general | solution.py:80
  123.0 3.4 %fusion.5 = f32[256,1280]{1,0:T(8,128)S(1)} fusion(f32[256,1280]{1,0:T(8,128)S(1)} %fusion.1, f32[256,1280]{1,0:T(8,128)S(1)} %fusion.2, bf16[256,1280]{1,0:T(8,128)(2,1)S(1)} %bitcast.75, bf16[3,1280,1280]{2,1,0:T(8,128)(2,1)} %all-gather.3.cloned.1.call-done), kind=kOutput, calls=%fused_computation.9 | convolution fusion | flops 839516160 | bytes 7864320 | tf_op jit(solution)/shard_map/dot_general | solution.py:80
  128.8 7.0 %all-to-all-start.2 = ((bf16[1,2,128,1280]{3,1,0,2:T(2,128)(2,1)}), bf16[1,2,128,1280]{3,1,0,2:T(2,128)(2,1)S(1)}, u32[]{:S(2)}, u32[]{:S(2)}) async-start(bf16[1,2,128,1280]{3,1,0,2:T(2,128)(2,1)} %copy.42), calls=%async_computation.2 | async-start | bytes 1310720 | tf_op jit(solution)/shard_map/all_to_all | solution.py:114
  136.0 10.7 %all-to-all-done.2 = bf16[1,2,128,1280]{3,1,0,2:T(2,128)(2,1)S(1)} async-done(((bf16[1,2,128,1280]{3,1,0,2:T(2,128)(2,1)}), bf16[1,2,128,1280]{3,1,0,2:T(2,128)(2,1)S(1)}, u32[]{:S(2)}, u32[]{:S(2)}) %all-to-all-start.2) | async-done | bytes 655392 | tf_op jit(solution)/shard_map/all_to_all | solution.py:114
  148.6 7.3 %all-to-all-start.6 = ((bf16[16,80,1280]{2,1,0:T(8,128)(2,1)}), bf16[16,80,1280]{2,1,0:T(8,128)(2,1)}, u32[]{:S(2)}, u32[]{:S(2)}) async-start(bf16[16,80,1280]{2,1,0:T(8,128)(2,1)} %stack.3), calls=%async_computation.6 | async-start | bytes 6553600 | tf_op jit(solution)/shard_map/all_to_all | solution.py:129
  156.0 63.8 %all-gather.5.cloned.1.call-done = bf16[1280,3840]{1,0:T(8,128)(2,1)} async-done(((bf16[80,3840]{1,0:T(8,128)(2,1)}), bf16[1280,3840]{1,0:T(8,128)(2,1)}) %all-gather.5.cloned.1.call-update) | async-done | bytes 9830416 | tf_op jit(solution)/shard_map/all_gather | solution.py:118
  219.8 6.5 %convolution_convert_fusion = bf16[256,3840]{1,0:T(8,128)(2,1)S(1)} fusion(bf16[256,1280]{1,0:T(8,128)(2,1)S(1)} %bitcast.77, bf16[1280,3840]{1,0:T(8,128)(2,1)} %all-gather.5.cloned.1.call-done), kind=kOutput, calls=%fused_computation.1 | convolution fusion | flops 2517565440 | bytes 12451840 | tf_op jit(solution)/shard_map/dot_general | solution.py:80
  226.3 4.5 %reshape_reshape.3 = bf16[1,32,8,3,20,64]{5,4,3,2,1,0:T(8,128)(2,1)} reshape(bf16[256,3840]{1,0:T(8,128)(2,1)S(1)} %convolution_convert_fusion) | data formatting | bytes 3932160 | tf_op jit(solution)/shard_map/reshape;reshape | solution.py:62
  230.7 3.3 %fusion.28 = (bf16[1,32,8,1,20,64]{5,4,3,2,1,0:T(8,128)(2,1)S(1)}, bf16[1,32,8,1,20,64]{5,4,3,2,1,0:T(8,128)(2,1)S(1)}, bf16[1,32,8,1,20,64]{5,4,3,2,1,0:T(8,128)(2,1)S(1)}) fusion(bf16[1,32,8,3,20,64]{5,4,3,2,1,0:T(8,128)(2,1)} %reshape_reshape.3), kind=kLoop, calls=%fused_computation.55 | loop fusion | bytes 3932160 | tf_op jit(solution)/shard_map/slice | solution.py:65
  235.7 6.0 %fusion.30 = (f32[8,20,32]{2,1,0:T(8,128)S(1)}, f32[8,20,32,32]{2,3,1,0:T(8,128)S(1)}) fusion(f32[8,20,32,32]{2,3,1,0:T(8,128)S(1)} %fusion.21), kind=kOutput, calls=%fused_computation.57 | output fusion | flops 655391 | bytes 1331200 | tf_op jit(solution)/shard_map/sub | solution.py:70
  244.4 31.3 %all_to_all.57 = bf16[1,32,8,1280]{3,2,0,1:T(8,128)(2,1)S(1)} all-to-all(bf16[1,32,8,1280]{3,2,0,1:T(8,128)(2,1)S(1)} %bitcast.74), channel_id=1, replica_groups=mesh['dp'=16,'frame_0'=4,'frame_1'=4] {'frame_0','frame_1'}, dimensions={1} | all-to-all | bytes 1310720 | tf_op jit(solution)/shard_map/all_to_all | solution.py:76
  275.8 3.8 %fusion.7 = bf16[1,2,128,1280]{3,2,1,0:T(8,128)(2,1)} fusion(bf16[1280,1280,1]{1,0,2:T(8,128)(2,1)} %bitcast.27, bf16[1,2,128,1280]{3,2,1,0:T(8,128)(2,1)S(1)} %get-tuple-element.6, bf16[1,2,16,8,1280]{4,3,1,2,0:T(8,128)(2,1)S(1)} %bitcast.78), kind=kOutput, calls=%fused_computation.14 | convolution fusion | flops 839843840 | bytes 5242880 | tf_op jit(solution)/shard_map/dot_general | solution.py:80
  (61 shorter events, 18.4 us)
Async XLA Ops:
  6.5 110.3 %all-gather.3.cloned.1.call-start = ((), (), s32[]{:S(2)}) async-start(), calls=%async_computation.7 | async-start | bytes 10444800 | tf_op jit(solution)/shard_map/all_gather | solution.py:103
  7.6 22.4 %copy-start.2 = (bf16[5,3840]{1,0:T(8,128)(2,1)S(1)}, bf16[5,3840]{1,0:T(8,128)(2,1)}, u32[]{:S(2)}) copy-start(bf16[5,3840]{1,0:T(8,128)(2,1)} %param.12) | copy-start | bytes 115204
  29.9 189.8 %all-gather.5.cloned.1.call-start = ((), (), s32[]{:S(2)}) async-start(), calls=%async_computation.8 | async-start | bytes 10444800 | tf_op jit(solution)/shard_map/all_gather | solution.py:118
  48.5 1.1 copy-start.3
  49.7 8.9 %copy-start = (bf16[1,2,128,1280]{3,2,1,0:T(8,128)(2,1)S(1)}, bf16[1,2,128,1280]{3,2,1,0:T(8,128)(2,1)}, u32[]{:S(2)}) copy-start(bf16[1,2,128,1280]{3,2,1,0:T(8,128)(2,1)} %param.7) | copy-start | bytes 1966084
  50.7 43.8 %copy-start.5 = (f32[1280]{0:T(1024)S(1)}, f32[1280]{0:T(1024)}, u32[]{:S(2)}) copy-start(f32[1280]{0:T(1024)} %param.9) | copy-start | bytes 15364
  50.7 57.4 %all-to-all-start.1 = ((bf16[16,20,1280]{2,1,0:T(8,128)(2,1)}), bf16[16,20,1280]{2,1,0:T(8,128)(2,1)S(1)}, u32[]{:S(2)}, u32[]{:S(2)}) async-start(bf16[16,20,1280]{2,1,0:T(8,128)(2,1)} %broadcast_in_dim.9), calls=%async_computation.1 | async-start | bytes 1966080 | tf_op jit(solution)/shard_map/all_to_all | solution.py:25
  95.0 13.1 %copy-start.4 = (bf16[5,1280]{1,0:T(8,128)(2,1)S(1)}, bf16[5,1280]{1,0:T(8,128)(2,1)}, u32[]{:S(2)}) copy-start(bf16[5,1280]{1,0:T(8,128)(2,1)} %param.13) | copy-start | bytes 38404
  95.0 7.5 %collective-permute-start = (bf16[1,1,128,1280]{3,2,1,0:T(8,128)(2,1)S(1)}, bf16[1,1,128,1280]{3,2,1,0:T(8,128)(2,1)S(1)}, u32[]{:S(2)}, u32[]{:S(2)}) collective-permute-start(bf16[1,1,128,1280]{3,2,1,0:T(8,128)(2,1)S(1)} %get-tuple-element.12), channel_id=1, source_target_pairs={{0,1},{1,2},{2,3},{3,4},{4,5},{5,6},{6,7},{7,8},{8,9},{9,10},{10,1... | collective-permute-start | bytes 983048 | tf_op jit(solution)/shard_map/ppermute | solution.py:45
  98.0 9.0 %collective-permute-start.1 = (bf16[1,1,128,1280]{3,2,1,0:T(8,128)(2,1)S(1)}, bf16[1,1,128,1280]{3,2,1,0:T(8,128)(2,1)S(1)}, u32[]{:S(2)}, u32[]{:S(2)}) collective-permute-start(bf16[1,1,128,1280]{3,2,1,0:T(8,128)(2,1)S(1)} %get-tuple-element.13), channel_id=1, source_target_pairs={{1,0},{2,1},{3,2},{4,3},{5,4},{6,5},{7,6},{8,7},{9,8},{10,9},{11,1... | collective-permute-start | bytes 983048 | tf_op jit(solution)/shard_map/ppermute | solution.py:46
  108.9 20.0 %all-to-all-start.5 = ((bf16[16,5,1280]{2,1,0:T(8,128)(2,1)}), bf16[16,5,1280]{2,1,0:T(8,128)(2,1)S(1)}, u32[]{:S(2)}, u32[]{:S(2)}) async-start(bf16[16,5,1280]{2,1,0:T(8,128)(2,1)} %broadcast_in_dim.11), calls=%async_computation.5 | async-start | bytes 655360 | tf_op jit(solution)/shard_map/all_to_all | solution.py:25
  120.0 3.0 %copy-start.1 = (bf16[1,2,128,1280]{3,2,1,0:T(8,128)(2,1)S(1)}, bf16[1,2,128,1280]{3,2,1,0:T(8,128)(2,1)}, u32[]{:S(2)}) copy-start(bf16[1,2,128,1280]{3,2,1,0:T(8,128)(2,1)} %get-tuple-element.10) | copy-start | bytes 1966084
  128.8 17.8 %all-to-all-start.2 = ((bf16[1,2,128,1280]{3,1,0,2:T(2,128)(2,1)}), bf16[1,2,128,1280]{3,1,0,2:T(2,128)(2,1)S(1)}, u32[]{:S(2)}, u32[]{:S(2)}) async-start(bf16[1,2,128,1280]{3,1,0,2:T(2,128)(2,1)} %copy.42), calls=%async_computation.2 | async-start | bytes 1310720 | tf_op jit(solution)/shard_map/all_to_all | solution.py:114
  148.6 95.9 %all-to-all-start.6 = ((bf16[16,80,1280]{2,1,0:T(8,128)(2,1)}), bf16[16,80,1280]{2,1,0:T(8,128)(2,1)}, u32[]{:S(2)}, u32[]{:S(2)}) async-start(bf16[16,80,1280]{2,1,0:T(8,128)(2,1)} %stack.3), calls=%async_computation.6 | async-start | bytes 6553600 | tf_op jit(solution)/shard_map/all_to_all | solution.py:129
Sparse Core Ops, SparseCore 0:
  30.0 81.5 all-gather.2
  113.5 106.2 all-gather.4
